TPU v7x, 256 devices: a whole 4x4x8 slice. The times are simulated.
256 devices in a mesh: rep: 64 (over z, y, core), shard: 4 (over x).
Axes of the slice: x: 4, y: 4, z: 8, core: 2. Of those that a mesh axis runs over, the one named last changes fastest.
Arguments:
- q_grad: float32 [64, 1152, 1152], P('rep', None, 'shard'), may hold values from -16 to 16
- o_grad: float32 [64, 1152, 1152], P('rep', None, 'shard'), may hold values from -16 to 16
- q_error: float32 [64, 1152, 1152], P('rep', None, 'shard'), may hold values from -4 to 4
- o_error: float32 [64, 1152, 1152], P('rep', None, 'shard'), may hold values from -4 to 4
- q_basis: float32 [1152, 32], P('shard'), may hold values from -6 to 6
- o_basis: float32 [1152, 32], P('shard'), may hold values from -6 to 6
- q_moment: float32 [1152, 1152], P('rep', 'shard'), may hold values from -6 to 6
- o_moment: float32 [1152, 1152], P('rep', 'shard'), may hold values from -6 to 6
- q_weight: float32 [1152, 1152], P('rep', 'shard'), may hold values from -0.1875 to 0.1875
- o_weight: float32 [1152, 1152], P('rep', 'shard'), may hold values from -0.1875 to 0.1875
- norm_grads: float32 [64, 4, 2304], P('rep', 'shard'), may hold values from -6 to 6
- norm_moment: float32 [2304], P(('rep', 'shard')), may hold values from -6 to 6
- norm_weight: float32 [2304], P(('rep', 'shard')), may hold values from 0.5 to 1.5
Outputs:
- q_weight_new: float32 [1152, 1152], P(None, 'shard')
- o_weight_new: float32 [1152, 1152], P(None, 'shard')
- q_moment_new: float32 [1152, 1152], P('rep', 'shard')
- o_moment_new: float32 [1152, 1152], P('rep', 'shard')
- q_error_new: float32 [64, 1152, 1152], P('rep', None, 'shard')
- o_error_new: float32 [64, 1152, 1152], P('rep', None, 'shard')
- norm_weight_new: float32 [2304], replicated
- norm_moment_new: float32 [2304], P(('rep', 'shard'))
All inputs are finite; a program needn't handle non-finite values.
Results may differ from a plain program's by a relative error of at most 0.0003.
Values sent between devices are 32-bit elements; how exact they have to be, the bound alone decides.
A program may use at most 64 MiB of HBM per device.

v0:
```python
import jax
import jax.numpy as jnp
from jax import lax
from jax.sharding import PartitionSpec as P

ROUNDS = 2
highest = lax.Precision.HIGHEST
decay_rate = 0.9
step_size = 0.1


def unwhiten(lower, factor):
    return jax.scipy.linalg.solve_triangular(lower, factor.T, lower=True).T


def product(left, right):
    return jnp.dot(left, right, precision=highest)


def per_device(
    q_grad,
    o_grad,
    q_error,
    o_error,
    q_basis,
    o_basis,
    q_moment,
    o_moment,
    q_weight,
    o_weight,
    norm_grads,
    norm_moment,
    norm_weight,
):
    corr_q = q_grad[0] + q_error[0]
    corr_o = o_grad[0] + o_error[0]
    basis_q = q_basis
    basis_o = o_basis
    normal_q = None
    normal_o = None
    for sweep in range(ROUNDS):
        part_q = product(corr_q, basis_q)
        part_o = product(corr_o, basis_o)
        left_q, left_o = lax.psum((part_q, part_o), ("rep", "shard"))
        gram_q = product(left_q.T, left_q)
        gram_o = product(left_o.T, left_o)
        lower_q = jnp.linalg.cholesky(gram_q)
        lower_o = jnp.linalg.cholesky(gram_o)
        normal_q = unwhiten(lower_q, left_q)
        normal_o = unwhiten(lower_o, left_o)
        reduce_q = product(corr_q.T, normal_q)
        reduce_o = product(corr_o.T, normal_o)
        summed_q, summed_o = lax.psum((reduce_q, reduce_o), "rep")
        basis_q = summed_q
        basis_o = summed_o
    decoded_q = product(normal_q, basis_q.T)
    decoded_o = product(normal_o, basis_o.T)
    q_error_new = (corr_q - decoded_q)[None]
    o_error_new = (corr_o - decoded_o)[None]
    row_count = q_moment.shape[0]
    start = lax.axis_index("rep") * row_count
    slice_q = lax.dynamic_slice_in_dim(decoded_q, start, row_count, 0)
    slice_o = lax.dynamic_slice_in_dim(decoded_o, start, row_count, 0)
    q_moment_new = decay_rate * q_moment + slice_q
    o_moment_new = decay_rate * o_moment + slice_o
    weight_q = q_weight - step_size * q_moment_new
    weight_o = o_weight - step_size * o_moment_new
    q_weight_new, o_weight_new = (
        lax.all_gather(weight_q, "rep", axis=0, tiled=True),
        lax.all_gather(weight_o, "rep", axis=0, tiled=True),
    )
    flat_grads = norm_grads.reshape(-1)
    norm_sum = lax.psum_scatter(flat_grads, ("rep", "shard"), scatter_dimension=0, tiled=True)
    norm_moment_new = decay_rate * norm_moment + norm_sum
    gain_share = norm_weight - step_size * norm_moment_new
    norm_weight_new = lax.all_gather(gain_share, ("rep", "shard"), axis=0, tiled=True)
    return (
        q_weight_new,
        o_weight_new,
        q_moment_new,
        o_moment_new,
        q_error_new,
        o_error_new,
        norm_weight_new,
        norm_moment_new,
    )


def solution(mesh):
    return jax.shard_map(
        per_device,
        mesh=mesh,
        in_specs=(
            P("rep", None, "shard"),
            P("rep", None, "shard"),
            P("rep", None, "shard"),
            P("rep", None, "shard"),
            P("shard", None),
            P("shard", None),
            P("rep", "shard"),
            P("rep", "shard"),
            P("rep", "shard"),
            P("rep", "shard"),
            P("rep", "shard", None),
            P(("rep", "shard")),
            P(("rep", "shard")),
        ),
        out_specs=(
            P(None, "shard"),
            P(None, "shard"),
            P("rep", "shard"),
            P("rep", "shard"),
            P("rep", None, "shard"),
            P("rep", None, "shard"),
            P(),
            P(("rep", "shard")),
        ),
        check_vma=False,
    )
```

profile of v0, /device:TPU:1, one launch (start us, length us, event | category | flops | bytes accessed | tf_op | source)
XLA Modules:
  0.0 1079.3 jit_solution(495348832060264353)
XLA Ops:
  7.2 2.0 add.52
  9.2 1.6 fusion.15
  11.6 1.6 fusion.6
  13.3 252.6 %all-reduce.13.cloned.1.call-done = (f32[1152,32]{0,1:T(8,128)}, f32[1152,32]{0,1:T(8,128)}) async-done(((f32[1152,32]{0,1:T(8,128)}, f32[1152,32]{0,1:T(8,128)}), (f32[1152,32]{0,1:T(8,128)}, f32[1152,32]{0,1:T(8,128)})) %all-reduce.13.cloned.1.call-update) | async-done | bytes 294928 | tf_op jit(solution)/shard_map/psum | solution.py:44
  265.9 1.3 fusion.40
  268.5 2.9 cholesky.96
  272.8 2.4 custom-call.10
  276.5 1.8 fusion.4
  278.4 2.9 cholesky.74
  282.7 2.4 custom-call.8
  285.5 1.8 fusion.13
  287.4 169.6 %all-reduce.17.cloned.1.call-done = (f32[288,32]{0,1:T(8,128)}, f32[288,32]{0,1:T(8,128)}) async-done(((f32[288,32]{0,1:T(8,128)}, f32[288,32]{0,1:T(8,128)}), (f32[288,32]{0,1:T(8,128)}, f32[288,32]{0,1:T(8,128)})) %all-reduce.17.cloned.1.call-update) | async-done | bytes 73744 | tf_op jit(solution)/shard_map/psum | solution.py:53
  457.0 2.4 fusion.11
  459.4 1.6 fusion.2
  461.3 247.8 %all-reduce.11.cloned.1.call-done = (f32[1152,32]{0,1:T(8,128)}, f32[1152,32]{0,1:T(8,128)}) async-done(((f32[1152,32]{0,1:T(8,128)}, f32[1152,32]{0,1:T(8,128)}), (f32[1152,32]{0,1:T(8,128)}, f32[1152,32]{0,1:T(8,128)})) %all-reduce.11.cloned.1.call-update) | async-done | bytes 294928 | tf_op jit(solution)/shard_map/psum | solution.py:44
  711.6 2.9 cholesky.107
  715.9 2.4 custom-call.11
  719.7 2.9 cholesky.85
  723.9 2.4 custom-call.9
  727.7 1.8 fusion.9
  729.5 1.8 fusion
  732.6 168.4 %all-reduce.15.cloned.1.call-done = (f32[288,32]{0,1:T(8,128)}, f32[288,32]{0,1:T(8,128)}) async-done(((f32[288,32]{0,1:T(8,128)}, f32[288,32]{0,1:T(8,128)}), (f32[288,32]{0,1:T(8,128)}, f32[288,32]{0,1:T(8,128)})) %all-reduce.15.cloned.1.call-update) | async-done | bytes 73744 | tf_op jit(solution)/shard_map/psum | solution.py:53
  901.0 2.1 fusion.42
  906.3 1.6 copy.54
  908.1 1.6 copy.49
  909.8 77.3 %all-reduce.1 = f32[2304]{0:T(1024)S(1)} all-reduce(f32[2304]{0:T(1024)S(1)} %reduce.4), channel_id=2, replica_groups=mesh['rep'=64,'shard'=4] {'rep','shard'}, use_global_device_ids=true, to_apply=%region_10.13.clone | all-reduce | flops 2304 | bytes 18432
  987.8 73.1 %all-reduce = f32[2304]{0:T(1024)} all-reduce(f32[2304]{0:T(1024)S(1)} %get-tuple-element.42), channel_id=1, replica_groups=mesh['rep'=64,'shard'=4] {'rep','shard'}, use_global_device_ids=true, to_apply=%add | all-reduce | flops 2304 | bytes 18432
  1062.3 3.5 fusion.8
  1065.8 1.7 reshape.35
  1067.6 1.6 copy.56
  1069.1 1.7 reshape.33
  1070.9 1.6 copy.55
  (87 shorter events, 21.3 us)
Async XLA Ops:
  7.2 2.0 copy-start
  7.2 258.7 %all-reduce.13.cloned.1.call-start = ((), (), s32[]{:S(2)}) async-start(), calls=%async_computation.3 | async-start | bytes 589824 | tf_op jit(solution)/shard_map/psum | solution.py:44
  7.2 3.6 copy-start.5
  9.2 1.6 copy-start.4
  10.8 0.8 copy-start.7
  13.2 443.8 %all-reduce.17.cloned.1.call-start = ((), (), s32[]{:S(2)}) async-start(), calls=%async_computation.5 | async-start | bytes 196608 | tf_op jit(solution)/shard_map/psum | solution.py:53
  265.9 19.2 %copy-start.3 = (f32[1152,32]{0,1:T(8,128)S(1)}, f32[1152,32]{0,1:T(8,128)}, u32[]{:S(2)}) copy-start(f32[1152,32]{0,1:T(8,128)} %get-tuple-element.36) | copy-start | bytes 442372
  287.4 421.7 %all-reduce.11.cloned.1.call-start = ((), (), s32[]{:S(2)}) async-start(), calls=%async_computation.2 | async-start | bytes 589824 | tf_op jit(solution)/shard_map/psum | solution.py:44
  457.0 2.4 copy-start.9
  461.0 440.0 %all-reduce.15.cloned.1.call-start = ((), (), s32[]{:S(2)}) async-start(), calls=%async_computation.4 | async-start | bytes 196608 | tf_op jit(solution)/shard_map/psum | solution.py:53
  727.6 3.8 copy-start.10
  727.7 3.9 copy-start.11
  729.5 2.2 copy-start.12
  729.5 2.3 copy-start.13
  731.4 334.4 %all-gather.7.cloned.1.call-start = ((), (), s32[]{:S(2)}) async-start(), calls=%async_computation.1 | async-start | bytes 2396160 | tf_op jit(solution)/shard_map/all_gather | solution.py:70
  901.0 2.1 copy-start.8
  901.0 4.4 copy-start.6
  903.1 3.2 copy-start.1
  904.4 1.1 copy-start.2
  905.5 4.3 copy-start.14
  905.5 81.7 %copy-start.15 = (f32[9]{0:T(128)S(1)}, f32[9]{0:T(128)}, u32[]{:S(2)}) copy-start(f32[9]{0:T(128)} %param.28) | copy-start | bytes 112
  905.5 81.7 %copy-start.16 = (f32[9]{0:T(128)S(1)}, f32[9]{0:T(128)}, u32[]{:S(2)}) copy-start(f32[9]{0:T(128)} %param.27) | copy-start | bytes 112
  908.0 161.1 %all-gather.5.cloned.1.call-start = ((), (), s32[]{:S(2)}) async-start(), calls=%async_computation | async-start | bytes 2396160 | tf_op jit(solution)/shard_map/all_gather | solution.py:69
Sparse Core Ops, SparseCore 0:
  14.2 251.6 all-reduce.12
  287.5 169.5 all-reduce.16
  463.2 245.7 all-reduce.10
  731.5 169.4 all-reduce.14
  908.1 75.9 all-gather.6
  986.6 75.1 all-gather.4
where the time goes:
time: 1080 us
  waiting for transfers between devices  839 us (78%)
  blocking collectives  150 us (14%)
  other arithmetic  33.9 us (3%)
  matrix products  27.1 us (3%)
  local copies, waits for them, and re-layouts  14.5 us (1%)
  between operations  14.4 us (1%)
    psum x2, waiting for transfers between devices, per_device(): left_q, left_o = lax.psum((part_q, part_o), ('rep', 'shard'))  500 us
    psum x2, waiting for transfers between devices, per_device(): summed_q, summed_o = lax.psum((reduce_q, reduce_o), 'rep')  338 us
    unnamed x2, blocking collectives  150 us
    dot_general x14, matrix products, product(): return jnp.dot(left, right, precision=highest)  22.9 us
  transfers between devices with their start and end apart: 6, of which 4 were waited for; matrix products, arithmetic and copies ran while one was open for 1% of the time, Pallas kernels for 0%

commit v1 on v0

--- a/solution.py
+++ b/solution.py
@@ -41,7 +41,7 @@
     for sweep in range(ROUNDS):
         part_q = product(corr_q, basis_q)
         part_o = product(corr_o, basis_o)
-        left_q, left_o = lax.psum((part_q, part_o), ("rep", "shard"))
+        left_q, left_o = lax.psum(lax.psum((part_q, part_o), "rep"), "shard")
         gram_q = product(left_q.T, left_q)
         gram_o = product(left_o.T, left_o)
         lower_q = jnp.linalg.cholesky(gram_q)

time: 1080 us -> 1040 us (0.963)
  waiting for transfers between devices: 839 us -> 799 us
    psum x2 -> x4, waiting for transfers between devices: 500 us -> 450 us  [per_device(): left_q, left_o = lax.psum(lax.psum((part_q, part_o), 'rep'), 'shard')]
  transfers between devices with their start and end apart: 6 -> 8, of which waited for: 4 -> 6; matrix products, arithmetic and copies ran while one was open for 1% -> 1% of each run, Pallas kernels for 0% -> 0%
where the time goes in v1:
time: 1040 us
  waiting for transfers between devices  799 us (77%)
  blocking collectives  151 us (15%)
  other arithmetic  33.9 us (3%)
  matrix products  27.1 us (3%)
  local copies, waits for them, and re-layouts  14.5 us (1%)
  between operations  14.5 us (1%)
    psum x4, waiting for transfers between devices, per_device(): left_q, left_o = lax.psum(lax.psum((part_q, part_o), 'rep'), 'shard')  450 us
    psum x2, waiting for transfers between devices, per_device(): summed_q, summed_o = lax.psum((reduce_q, reduce_o), 'rep')  349 us
    unnamed x2, blocking collectives  151 us
    dot_general x14, matrix products, product(): return jnp.dot(left, right, precision=highest)  22.9 us
  transfers between devices with their start and end apart: 8, of which 6 were waited for; matrix products, arithmetic and copies ran while one was open for 1% of the time, Pallas kernels for 0%

profile of v1, /device:TPU:1, one launch (start us, length us, event | category | flops | bytes accessed | tf_op | source)
XLA Modules:
  0.0 1040.1 jit_solution(683632882342365693)
XLA Ops:
  7.2 2.0 add.60
  9.2 1.6 fusion.15
  11.6 1.6 fusion.6
  13.3 182.2 %all-reduce.21.cloned.1.call-done = (f32[1152,32]{0,1:T(8,128)}, f32[1152,32]{0,1:T(8,128)}) async-done(((f32[1152,32]{0,1:T(8,128)}, f32[1152,32]{0,1:T(8,128)}), (f32[1152,32]{0,1:T(8,128)}, f32[1152,32]{0,1:T(8,128)})) %all-reduce.21.cloned.1.call-update) | async-done | bytes 294928 | tf_op jit(solution)/shard_map/psum | solution.py:44
  195.6 46.1 %all-reduce.25.cloned.1.call-done = (f32[1152,32]{0,1:T(8,128)}, f32[1152,32]{0,1:T(8,128)}) async-done(((f32[1152,32]{0,1:T(8,128)}, f32[1152,32]{0,1:T(8,128)}), (f32[1152,32]{0,1:T(8,128)}, f32[1152,32]{0,1:T(8,128)})) %all-reduce.25.cloned.1.call-update) | async-done | bytes 294928 | tf_op jit(solution)/shard_map/psum | solution.py:44
  244.3 2.9 cholesky.96
  248.6 2.4 custom-call.10
  252.3 1.8 fusion.4
  254.2 2.9 cholesky.74
  258.5 2.4 custom-call.8
  261.3 1.8 fusion.13
  263.2 174.9 %all-reduce.17.cloned.1.call-done = (f32[288,32]{0,1:T(8,128)}, f32[288,32]{0,1:T(8,128)}) async-done(((f32[288,32]{0,1:T(8,128)}, f32[288,32]{0,1:T(8,128)}), (f32[288,32]{0,1:T(8,128)}, f32[288,32]{0,1:T(8,128)})) %all-reduce.17.cloned.1.call-update) | async-done | bytes 73744 | tf_op jit(solution)/shard_map/psum | solution.py:53
  438.1 2.4 fusion.11
  440.5 1.6 fusion.2
  442.1 176.3 %all-reduce.19.cloned.1.call-done = (f32[1152,32]{0,1:T(8,128)}, f32[1152,32]{0,1:T(8,128)}) async-done(((f32[1152,32]{0,1:T(8,128)}, f32[1152,32]{0,1:T(8,128)}), (f32[1152,32]{0,1:T(8,128)}, f32[1152,32]{0,1:T(8,128)})) %all-reduce.19.cloned.1.call-update) | async-done | bytes 294928 | tf_op jit(solution)/shard_map/psum | solution.py:44
  618.7 45.8 %all-reduce.23.cloned.1.call-done = (f32[1152,32]{0,1:T(8,128)}, f32[1152,32]{0,1:T(8,128)}) async-done(((f32[1152,32]{0,1:T(8,128)}, f32[1152,32]{0,1:T(8,128)}), (f32[1152,32]{0,1:T(8,128)}, f32[1152,32]{0,1:T(8,128)})) %all-reduce.23.cloned.1.call-update) | async-done | bytes 294928 | tf_op jit(solution)/shard_map/psum | solution.py:44
  667.1 2.9 cholesky.107
  671.3 2.4 custom-call.11
  675.1 2.9 cholesky.85
  679.4 2.4 custom-call.9
  683.1 1.8 fusion.9
  685.0 1.8 fusion
  688.0 173.7 %all-reduce.15.cloned.1.call-done = (f32[288,32]{0,1:T(8,128)}, f32[288,32]{0,1:T(8,128)}) async-done(((f32[288,32]{0,1:T(8,128)}, f32[288,32]{0,1:T(8,128)}), (f32[288,32]{0,1:T(8,128)}, f32[288,32]{0,1:T(8,128)})) %all-reduce.15.cloned.1.call-update) | async-done | bytes 73744 | tf_op jit(solution)/shard_map/psum | solution.py:53
  861.8 2.1 fusion.42
  867.1 1.6 copy.54
  868.8 1.6 copy.49
  870.5 77.3 %all-reduce.1 = f32[2304]{0:T(1024)S(1)} all-reduce(f32[2304]{0:T(1024)S(1)} %reduce.4), channel_id=2, replica_groups=mesh['rep'=64,'shard'=4] {'rep','shard'}, use_global_device_ids=true, to_apply=%region_14.17.clone | all-reduce | flops 2304 | bytes 18432
  948.5 73.2 %all-reduce = f32[2304]{0:T(1024)} all-reduce(f32[2304]{0:T(1024)S(1)} %get-tuple-element.46), channel_id=1, replica_groups=mesh['rep'=64,'shard'=4] {'rep','shard'}, use_global_device_ids=true, to_apply=%add | all-reduce | flops 2304 | bytes 18432
  1023.2 3.5 fusion.8
  1026.6 1.7 reshape.35
  1028.4 1.6 copy.56
  1030.0 1.7 reshape.33
  (93 shorter events, 24.3 us)
Async XLA Ops:
  7.2 2.0 copy-start
  7.2 188.3 %all-reduce.21.cloned.1.call-start = ((), (), s32[]{:S(2)}) async-start(), calls=%async_computation.5 | async-start | bytes 589824 | tf_op jit(solution)/shard_map/psum | solution.py:44
  7.2 3.6 copy-start.5
  9.2 1.6 copy-start.4
  10.8 0.8 copy-start.7
  13.2 228.4 %all-reduce.25.cloned.1.call-start = ((), (), s32[]{:S(2)}) async-start(), calls=%async_computation.7 | async-start | bytes 589824 | tf_op jit(solution)/shard_map/psum | solution.py:44
  195.5 242.5 %all-reduce.17.cloned.1.call-start = ((), (), s32[]{:S(2)}) async-start(), calls=%async_computation.3 | async-start | bytes 196608 | tf_op jit(solution)/shard_map/psum | solution.py:53
  241.7 19.2 %copy-start.3 = (f32[1152,32]{0,1:T(8,128)S(1)}, f32[1152,32]{0,1:T(8,128)}, u32[]{:S(2)}) copy-start(f32[1152,32]{0,1:T(8,128)} %get-tuple-element.44) | copy-start | bytes 442372
  263.1 355.3 %all-reduce.19.cloned.1.call-start = ((), (), s32[]{:S(2)}) async-start(), calls=%async_computation.4 | async-start | bytes 589824 | tf_op jit(solution)/shard_map/psum | solution.py:44
  438.1 2.4 copy-start.9
  442.1 222.4 %all-reduce.23.cloned.1.call-start = ((), (), s32[]{:S(2)}) async-start(), calls=%async_computation.6 | async-start | bytes 589824 | tf_op jit(solution)/shard_map/psum | solution.py:44
  618.5 243.3 %all-reduce.15.cloned.1.call-start = ((), (), s32[]{:S(2)}) async-start(), calls=%async_computation.2 | async-start | bytes 196608 | tf_op jit(solution)/shard_map/psum | solution.py:53
  683.1 3.8 copy-start.10
  683.1 3.9 copy-start.11
  685.0 2.2 copy-start.12
  685.0 2.3 copy-start.13
  686.8 339.8 %all-gather.7.cloned.1.call-start = ((), (), s32[]{:S(2)}) async-start(), calls=%async_computation.1 | async-start | bytes 2396160 | tf_op jit(solution)/shard_map/all_gather | solution.py:70
  861.8 2.1 copy-start.8
  861.8 4.4 copy-start.6
  863.9 3.2 copy-start.1
  865.1 1.1 copy-start.2
  866.2 4.3 copy-start.14
  866.2 81.7 %copy-start.15 = (f32[9]{0:T(128)S(1)}, f32[9]{0:T(128)}, u32[]{:S(2)}) copy-start(f32[9]{0:T(128)} %param.28) | copy-start | bytes 112
  866.2 81.7 %copy-start.16 = (f32[9]{0:T(128)S(1)}, f32[9]{0:T(128)}, u32[]{:S(2)}) copy-start(f32[9]{0:T(128)} %param.27) | copy-start | bytes 112
  868.7 161.2 %all-gather.5.cloned.1.call-start = ((), (), s32[]{:S(2)}) async-start(), calls=%async_computation | async-start | bytes 2396160 | tf_op jit(solution)/shard_map/all_gather | solution.py:69
Sparse Core Ops, SparseCore 0:
  13.4 182.1 all-reduce.20
  197.9 43.7 all-reduce.24
  263.3 174.7 all-reduce.16
  442.2 176.2 all-reduce.18
  620.7 43.7 all-reduce.22
  686.9 174.7 all-reduce.14
  868.9 75.9 all-gather.6
  947.5 75.0 all-gather.4
